TPU v7x, 256 devices: a whole 4x4x8 slice. The times are simulated.
256 devices in a mesh: src: 32 (over z, y), obs: 8 (over x, core).
Axes of the slice: x: 4, y: 4, z: 8, core: 2. Of those that a mesh axis runs over, the one named last changes fastest.
Arguments:
- tiles: bfloat16 [32, 8, 8, 8, 128, 128], P('src', 'obs'), may hold values from -0.125 to 0.125
- tile_src: int32 [32, 8, 8], P('src', 'obs'), may hold values from 0 to 7
- tile_obs: int32 [32, 8, 8], P('src', 'obs'), may hold values from 0 to 31
- tile_off: int32 [32, 8, 8], P('src', 'obs'), may hold values from 0 to 32, as said below
- history: bfloat16 [8, 1, 32, 40, 32, 128], P(None, None, 'src'), may hold values from -6 to 6
- excitation: bfloat16 [2, 8, 1, 32, 32, 128], P(None, 'obs', None, 'src'), may hold values from -6 to 6
- inverse: bfloat16 [8, 1, 32, 128, 128], P('obs', None, 'src'), may hold values from -0.5 to 0.5
Outputs:
- currents: bfloat16 [2, 8, 1, 32, 32, 128], P(None, 'obs', None, 'src')
Inputs may be any that keep to these rules, and one draw needn't show every extreme that they name: `tile_off`: the delay offset of every tile; the least and the largest offset occur in every draw.
All inputs are finite; a program needn't handle non-finite values.
Results may differ from a plain program's by a relative error of at most 0.012.
Values may be sent and summed in bfloat16 or wider, within the bound.
A program may use at most 64 MiB of HBM per device.

v0:
```python
import jax
import jax.numpy as jnp
from jax import lax
from jax.sharding import PartitionSpec as P

G = 128
R = 32
HIST = 40
TAPS = 8
STEPS = 2


def local(tiles, tile_src, tile_obs, tile_off, history, excitation, inverse):
    zero = jnp.zeros((), jnp.int32)
    n_source = lax.axis_size("src")
    n_observer = lax.axis_size("obs")
    owned = history.shape[1]
    hist = history.reshape(n_observer * owned, HIST, R, G)
    blocks = tiles[0, 0]
    sources = tile_src[0, 0]
    targets = tile_obs[0, 0]
    offsets = tile_off[0, 0]
    onehot = (targets[:, None] == jnp.arange(n_source * owned, dtype=jnp.int32)[None, :]).astype(
        jnp.float32
    )
    inv_blocks = inverse[0, :, 0]

    def window(j_index, offset):
        return lax.dynamic_slice(hist_now[0], (j_index, offset, zero, zero), (1, TAPS, R, G))[0]

    results = []
    hist_now = [hist]
    for step in range(STEPS):
        windows = jax.vmap(window)(sources, offsets)
        contrib = jnp.einsum("targ,tagh->trh", windows, blocks, preferred_element_type=jnp.float32)
        mine = lax.psum_scatter(
            jnp.einsum("ti,trh->irh", onehot, contrib), "src", scatter_dimension=0, tiled=True
        )
        field = (excitation[step, 0, :, 0].astype(jnp.float32) - mine).astype(jnp.bfloat16)
        newer = jnp.einsum(
            "krg,kgh->krh", field, inv_blocks, preferred_element_type=jnp.float32
        ).astype(jnp.bfloat16)
        results.append(newer)
        arrived = lax.all_gather(newer, "obs", axis=0, tiled=True)
        hist_now[0] = jnp.concatenate([arrived[:, None], hist_now[0][:, :-1]], axis=1)
    stacked = jnp.stack(results)
    return stacked.reshape(STEPS, 1, owned, 1, R, G)


def solution(mesh):
    placed = (
        P("src", "obs", None, None, None, None),
        P("src", "obs", None),
        P("src", "obs", None),
        P("src", "obs", None),
        P(None, None, "src", None, None, None),
        P(None, "obs", None, "src", None, None),
        P("obs", None, "src", None, None),
    )
    return jax.shard_map(
        local,
        mesh=mesh,
        in_specs=placed,
        out_specs=P(None, "obs", None, "src", None, None),
        check_vma=False,
    )
```

profile of v0, /device:TPU:32, one launch (start us, length us, event | category | flops | bytes accessed | tf_op | source)
XLA Modules:
  0.0 477.5 jit_solution(3326985576628295378)
XLA Ops:
  6.5 0.0 copy-start
  6.5 0.0 copy-start.4
  6.5 0.0 copy-start.5
  6.5 0.0 reduce-scatter.3.cloned.1.call-start
  6.5 4.2 copy.25
  10.8 0.0 copy-done.4
  10.8 0.0 copy-done.5
  10.8 2.4 gather_fusion
  13.2 0.0 copy-done
  13.2 0.5 fusion.4
  13.7 0.0 copy-done.3
  13.7 0.3 fusion.13
  14.0 1.1 copy.14
  15.1 0.0 reduce-scatter.3.cloned.1.call-update
  15.2 0.0 copy-start.1
  15.2 0.0 copy-start.2
  15.2 0.0 reduce-scatter.5.cloned.1.call-start
  15.2 4.0 slice.24
  19.2 214.1 %reduce-scatter.3.cloned.1.call-done = f32[1,32,128]{2,1,0:T(8,128)} async-done(((f32[32,32,128]{2,1,0:T(8,128)}), f32[1,32,128]{2,1,0:T(8,128)}) %reduce-scatter.3.cloned.1.call-update) | async-done | bytes 16400 | tf_op jit(solution)/shard_map/reduce_scatter | solution.py:36
  233.3 0.0 copy-done.1
  233.3 0.0 copy-done.2
  233.3 0.8 convolution_convert_fusion.1
  234.2 13.1 %all-gather = bf16[256,128]{1,0:T(8,128)(2,1)S(1)} all-gather(bf16[32,128]{1,0:T(8,128)(2,1)S(1)} %convolution_convert_fusion.1), channel_id=2, replica_groups=mesh['src'=32,'obs'=8] {'obs'}, dimensions={0}, use_global_device_ids=true | all-gather | bytes 73728 | tf_op jit(solution)/shard_map/all_gather | solution.py:44
  247.2 3.5 pad_maximum_fusion
  250.7 2.4 gather_fusion.1
  253.1 0.5 fusion.7
  253.6 0.3 fusion.11
  253.9 1.1 copy.16
  255.0 0.0 reduce-scatter.5.cloned.1.call-update
  255.0 214.2 %reduce-scatter.5.cloned.1.call-done = f32[1,32,128]{2,1,0:T(8,128)} async-done(((f32[32,32,128]{2,1,0:T(8,128)}), f32[1,32,128]{2,1,0:T(8,128)}) %reduce-scatter.5.cloned.1.call-update) | async-done | bytes 16400 | tf_op jit(solution)/shard_map/reduce_scatter | solution.py:36
  469.2 0.8 fusion.10
  470.1 0.6 maximum_bitcast_fusion
  (2 shorter events, 0.0 us)
Async XLA Ops:
  6.5 6.6 %copy-start = (bf16[1,1,8,8,128,128]{5,4,3,2,1,0:T(8,128)(2,1)S(1)}, bf16[1,1,8,8,128,128]{5,4,3,2,1,0:T(8,128)(2,1)}, u32[]{:S(2)}) copy-start(bf16[1,1,8,8,128,128]{5,4,3,2,1,0:T(8,128)(2,1)} %param.7) | copy-start | bytes 6291460
  6.5 4.2 copy-start.4
  6.5 4.2 copy-start.5
  6.5 226.8 %reduce-scatter.3.cloned.1.call-start = ((), (), s32[]{:S(2)}) async-start(), calls=%async_computation.2 | async-start | bytes 540672 | tf_op jit(solution)/shard_map/reduce_scatter | solution.py:36
  10.8 2.9 copy-start.3
  15.2 218.2 %copy-start.1 = (bf16[1,1,1,128,128]{4,3,2,1,0:T(8,128)(2,1)S(1)}, bf16[1,1,1,128,128]{4,3,2,1,0:T(8,128)(2,1)}, u32[]{:S(2)}) copy-start(bf16[1,1,1,128,128]{4,3,2,1,0:T(8,128)(2,1)} %param.13) | copy-start | bytes 98308
  15.2 218.1 %copy-start.2 = (bf16[2,1,1,1,32,128]{5,4,3,2,1,0:T(8,128)(2,1)S(1)}, bf16[2,1,1,1,32,128]{5,4,3,2,1,0:T(8,128)(2,1)}, u32[]{:S(2)}) copy-start(bf16[2,1,1,1,32,128]{5,4,3,2,1,0:T(8,128)(2,1)} %param.12) | copy-start | bytes 49156
  15.2 454.0 %reduce-scatter.5.cloned.1.call-start = ((), (), s32[]{:S(2)}) async-start(), calls=%async_computation.3 | async-start | bytes 540672 | tf_op jit(solution)/shard_map/reduce_scatter | solution.py:36
Sparse Core Ops, SparseCore 0:
  15.3 217.9 reduce-scatter.2
  255.2 214.0 reduce-scatter.4
where the time goes:
time: 479 us; the launch traced here: 478 us
  waiting for transfers between devices  428 us (89%)
  local copies, waits for them, and re-layouts  15.2 us (3%)
  between operations  13.5 us (3%)
  blocking collectives  13.1 us (3%)
    reduce_scatter x2, waiting for transfers between devices, local(): lax.psum_scatter(jnp.einsum('ti,trh->irh', onehot, contrib), 'src', scatt...  428 us
    all_gather x1, blocking collectives, local(): arrived = lax.all_gather(newer, 'obs', axis=0, tiled=True)  13.1 us
  transfers between devices with their start and end apart: 2, of which 2 were waited for; matrix products, arithmetic and copies ran while one was open for 1% of the time, Pallas kernels for 0%

commit v1 on v0

v1 whole, which is shorter than its diff:
```python
import jax
import jax.numpy as jnp
from jax import lax
from jax.experimental import pallas as pl
from jax.experimental.pallas import tpu as pltpu
from jax.sharding import PartitionSpec as P

G = 128
R = 32
HIST = 40
TAPS = 8
STEPS = 2
TILES = 8
NZ = 8
NY = 4
NO = 8
MESH = pl.DeviceIdType.MESH

DELTA = (4, 3, 5, 2, 6, 1, 7, 0)
PER = 2
CHUNKS = NZ // PER
NEAR = NZ - 1
Y_ORDER = (2, 1, 3)
O_ORDER = (4, 5, 2, 3, 6, 7, 1)


def kernel(
    tiles_hbm, src_ref, obs_ref, off_ref, hist_hbm, exc_hbm, inv_hbm, out_ref,
    tiles, hist, exc, inv, contrib, part, mine, y_in, z_out, z_in, news,
    load_sem, hist_sem, tile_sem, y_send, y_recv, z_send, z_recv, o_send, o_recv,
):
    src = lax.axis_index("src")
    obs = lax.axis_index("obs")
    z = lax.div(src, NY)
    y = lax.rem(src, NY)

    def y_peer(d):
        return z * NY + lax.rem(y + d, NY)

    def z_peer(k):
        return lax.rem(z + DELTA[k], NZ) * NY + y

    def o_peer(e):
        return lax.rem(obs + e, NO)

    loads = []
    for j in range(NO):
        loads.append(pltpu.make_async_copy(hist_hbm.at[j], hist.at[j], hist_sem.at[j]))
    for t in range(TILES):
        loads.append(pltpu.make_async_copy(tiles_hbm.at[t], tiles.at[t], tile_sem.at[t]))
    loads.append(pltpu.make_async_copy(exc_hbm, exc, load_sem.at[0]))
    loads.append(pltpu.make_async_copy(inv_hbm, inv, load_sem.at[1]))
    for load in loads:
        load.start()

    barrier = pltpu.get_barrier_semaphore()
    for k in range(NEAR):
        pl.semaphore_signal(barrier, inc=1, device_id={"src": z_peer(k)}, device_id_type=MESH)
    for d in Y_ORDER:
        pl.semaphore_signal(barrier, inc=1, device_id={"src": y_peer(d)}, device_id_type=MESH)
    for e in O_ORDER:
        pl.semaphore_signal(barrier, inc=1, device_id={"obs": o_peer(e)}, device_id_type=MESH)

    for load in loads:
        load.wait()

    def block(t):
        return tiles[t].reshape(TAPS * G, G)

    for t in range(TILES):
        seen = hist[src_ref[t], pl.ds(off_ref[t], TAPS)]
        wide = jnp.concatenate([seen[p] for p in range(TAPS)], axis=1)
        contrib[0, t] = jnp.dot(wide, block(t), preferred_element_type=jnp.float32)

    pl.semaphore_wait(barrier, NEAR + NY - 1 + NO - 1)

    def y_copy(step, chunk, d):
        span = pl.ds(chunk * PER, PER)
        return pltpu.make_async_remote_copy(
            src_ref=part.at[step, d - 1, span],
            dst_ref=y_in.at[step, d - 1, span],
            send_sem=y_send.at[step, chunk, d - 1],
            recv_sem=y_recv.at[step, chunk, d - 1],
            device_id={"src": y_peer(d)},
            device_id_type=MESH,
        )

    def z_copy(step, k):
        return pltpu.make_async_remote_copy(
            src_ref=z_out.at[step, k],
            dst_ref=z_in.at[step, k],
            send_sem=z_send.at[step, k],
            recv_sem=z_recv.at[step, k],
            device_id={"src": z_peer(k)},
            device_id_type=MESH,
        )

    def o_copy(e):
        return pltpu.make_async_remote_copy(
            src_ref=news.at[obs],
            dst_ref=news.at[obs],
            send_sem=o_send.at[e - 1],
            recv_sem=o_recv.at[e - 1],
            device_id={"obs": o_peer(e)},
            device_id_type=MESH,
        )

    def owned_sum(step, owner):
        total = jnp.where(obs_ref[0] == owner, contrib[step, 0], 0.0)
        for t in range(1, TILES):
            total = total + jnp.where(obs_ref[t] == owner, contrib[step, t], 0.0)
        return total

    def scatter(step):
        for chunk in range(CHUNKS):
            for d in Y_ORDER:
                for k in range(chunk * PER, chunk * PER + PER):
                    owner = lax.rem(z + DELTA[k], NZ) * NY + lax.rem(y + d, NY)
                    part[step, d - 1, k] = owned_sum(step, owner).astype(jnp.bfloat16)
                y_copy(step, chunk, d).start()
        for k in range(NZ):
            mine[step, k] = owned_sum(step, lax.rem(z + DELTA[k], NZ) * NY + y)

    def gather_sum(step):
        for chunk in range(CHUNKS):
            for d in Y_ORDER:
                y_copy(step, chunk, d).wait_recv()
            for k in range(chunk * PER, chunk * PER + PER):
                total = mine[step, k]
                for d in Y_ORDER:
                    total = total + y_in[step, d - 1, k].astype(jnp.float32)
                if k < NEAR:
                    z_out[step, k] = total.astype(jnp.bfloat16)
                    z_copy(step, k).start()
        for k in range(NEAR - 1, -1, -1):
            z_copy(step, k).wait_recv()
            total = total + z_in[step, k].astype(jnp.float32)
        return total

    def solve(step, scattered):
        field = (exc[step].astype(jnp.float32) - scattered).astype(jnp.bfloat16)
        newer = jnp.dot(field, inv[...], preferred_element_type=jnp.float32).astype(jnp.bfloat16)
        out_ref[step] = newer
        return newer

    scatter(0)
    for t in range(TILES):
        off = off_ref[t]
        before = hist[src_ref[t], pl.ds(jnp.maximum(off - 1, 0), 1)][0]
        before = jnp.where(off > 0, before, jnp.zeros_like(before))
        seen = hist[src_ref[t], pl.ds(off, TAPS - 1)]
        wide = jnp.concatenate([before] + [seen[p] for p in range(TAPS - 1)], axis=1)
        contrib[1, t] = jnp.dot(wide, block(t), preferred_element_type=jnp.float32)

    news[obs] = solve(0, gather_sum(0))
    for e in O_ORDER:
        o_copy(e).start()
    for e in O_ORDER:
        o_copy(e).wait_recv()
    for t in range(TILES):
        fresh = news[src_ref[t]]
        fresh = jnp.where(off_ref[t] == 0, fresh, jnp.zeros_like(fresh))
        contrib[1, t] += jnp.dot(fresh, tiles[t, 0], preferred_element_type=jnp.float32)
    scatter(1)
    solve(1, gather_sum(1))

    for step in range(STEPS):
        for chunk in range(CHUNKS):
            for d in Y_ORDER:
                y_copy(step, chunk, d).wait_send()
        for k in range(NEAR):
            z_copy(step, k).wait_send()
    for e in O_ORDER:
        o_copy(e).wait_send()


def local(tiles, tile_src, tile_obs, tile_off, history, excitation, inverse):
    hbm = pl.BlockSpec(memory_space=pl.ANY)
    smem = pl.BlockSpec(memory_space=pltpu.SMEM)
    bf16, f32 = jnp.bfloat16, jnp.float32
    dma = pltpu.SemaphoreType.DMA
    out = pl.pallas_call(
        kernel,
        out_shape=jax.ShapeDtypeStruct((STEPS, R, G), bf16),
        in_specs=[hbm, smem, smem, smem, hbm, hbm, hbm],
        out_specs=pl.BlockSpec(memory_space=pltpu.VMEM),
        scratch_shapes=[
            pltpu.VMEM((TILES, TAPS, G, G), bf16),
            pltpu.VMEM((NO, HIST, R, G), bf16),
            pltpu.VMEM((STEPS, R, G), bf16),
            pltpu.VMEM((G, G), bf16),
            pltpu.VMEM((STEPS, TILES, R, G), f32),
            pltpu.VMEM((STEPS, NY - 1, NZ, R, G), bf16),
            pltpu.VMEM((STEPS, NZ, R, G), f32),
            pltpu.VMEM((STEPS, NY - 1, NZ, R, G), bf16),
            pltpu.VMEM((STEPS, NEAR, R, G), bf16),
            pltpu.VMEM((STEPS, NEAR, R, G), bf16),
            pltpu.VMEM((NO, R, G), bf16),
            dma((2,)),
            dma((NO,)),
            dma((TILES,)),
            dma((STEPS, CHUNKS, NY - 1)),
            dma((STEPS, CHUNKS, NY - 1)),
            dma((STEPS, NEAR)),
            dma((STEPS, NEAR)),
            dma((NO - 1,)),
            dma((NO - 1,)),
        ],
        compiler_params=pltpu.CompilerParams(collective_id=0, has_side_effects=True),
        name="march",
    )(
        tiles.reshape(TILES, TAPS, G, G),
        tile_src.reshape(TILES),
        tile_obs.reshape(TILES),
        tile_off.reshape(TILES),
        history.reshape(NO, HIST, R, G),
        excitation.reshape(STEPS, R, G),
        inverse.reshape(G, G),
    )
    return out.reshape(STEPS, 1, 1, 1, R, G)


def solution(mesh):
    placed = (
        P("src", "obs", None, None, None, None),
        P("src", "obs", None),
        P("src", "obs", None),
        P("src", "obs", None),
        P(None, None, "src", None, None, None),
        P(None, "obs", None, "src", None, None),
        P("obs", None, "src", None, None),
    )
    return jax.shard_map(
        local,
        mesh=mesh,
        in_specs=placed,
        out_specs=P(None, "obs", None, "src", None, None),
        check_vma=False,
    )
```

time: 479 us -> 33.4 us (0.07)
  waiting for transfers between devices: 428 us -> 0 us
  Pallas kernels: 0 us -> 31.9 us
  local copies, waits for them, and re-layouts: 15.2 us -> 1.32 us
  between operations: 13.5 us -> 0.01 us
  blocking collectives: 13.1 us -> 0 us
    reduce_scatter x2 -> x0, waiting for transfers between devices: 428 us -> none  [local(): lax.psum_scatter(jnp.einsum('ti,trh->irh', onehot, contrib), 'src', scatt...]
    pallas_call x0 -> x1, Pallas kernels: none -> 31.9 us  [local(): pl.pallas_call(kernel, out_shape=jax.ShapeDtypeStruct((STEPS, R, G), bf16...]
    all_gather x1 -> x0, blocking collectives: 13.1 us -> none  [local(): arrived = lax.all_gather(newer, 'obs', axis=0, tiled=True)]
  transfers between devices with their start and end apart: 2 -> 0, of which waited for: 2 -> 0; matrix products, arithmetic and copies ran while one was open for 1% -> 0% of each run, Pallas kernels for 0% -> 0%
where the time goes in v1:
time: 33.4 us; the launch traced here: 33.2 us
  Pallas kernels  31.9 us (96%)
  local copies, waits for them, and re-layouts  1.32 us (4%)
    pallas_call x1, Pallas kernels, local(): pl.pallas_call(kernel, out_shape=jax.ShapeDtypeStruct((STEPS, R, G), bf16...  31.9 us
    unnamed x1, local copies, waits for them, and re-layouts  1.32 us

profile of v1, /device:TPU:32, one launch (start us, length us, event | category | flops | bytes accessed | tf_op | source)
XLA Modules:
  0.0 33.2 jit_solution(14196315171358639928)
XLA Ops:
  0.0 31.9 %march.1 = bf16[2,32,128]{2,1,0:T(8,128)(2,1)} custom-call(bf16[8,8,128,128]{3,2,1,0:T(8,128)(2,1)} %bitcast.11, s32[8]{0:T(128)} %bitcast.15, s32[8]{0:T(128)} %bitcast.16, s32[8]{0:T(128)} %bitcast.17, bf16[8,40,32,128]{3,2,1,0:T(8,128)(2,1)} %bitcast.10, bf16[2,32,128]{2,1,0:T(8,128)(2,1)} %bitcast.14, bf16[128,128]{1,0:T(8,128)(2,1)} %bitcast.13), custom_call_target="tpu_custom_call" | custom-call | tf_op jit(solution)/shard_map/march/pallas_call | solution.py:182
  31.9 1.3 %copy.10 = bf16[2,1,1,1,32,128]{5,4,3,2,1,0:T(8,128)(2,1)} copy(bf16[2,1,1,1,32,128]{5,4,3,2,1,0:T(8,128)(2,1)} %bitcast.12) | data formatting | bytes 32768

commit v2 on v1

--- a/solution.py
+++ b/solution.py
@@ -25,8 +25,8 @@
 
 
 def kernel(
-    tiles_hbm, src_ref, obs_ref, off_ref, hist_hbm, exc_hbm, inv_hbm, out_ref,
-    tiles, hist, exc, inv, contrib, part, mine, y_in, z_out, z_in, news,
+    tiles_hbm, src_hbm, obs_hbm, off_hbm, hist_hbm, exc_hbm, inv_hbm, out_ref,
+    src_ref, obs_ref, off_ref, tiles, hist, exc, inv, contrib, part, mine, y_in, z_out, z_in, news,
     load_sem, hist_sem, tile_sem, y_send, y_recv, z_send, z_recv, o_send, o_recv,
 ):
     src = lax.axis_index("src")
@@ -43,7 +43,11 @@
     def o_peer(e):
         return lax.rem(obs + e, NO)
 
-    loads = []
+    loads = [
+        pltpu.make_async_copy(src_hbm, src_ref, load_sem.at[2]),
+        pltpu.make_async_copy(obs_hbm, obs_ref, load_sem.at[3]),
+        pltpu.make_async_copy(off_hbm, off_ref, load_sem.at[4]),
+    ]
     for j in range(NO):
         loads.append(pltpu.make_async_copy(hist_hbm.at[j], hist.at[j], hist_sem.at[j]))
     for t in range(TILES):
@@ -175,16 +179,19 @@
 
 
 def local(tiles, tile_src, tile_obs, tile_off, history, excitation, inverse):
-    hbm = pl.BlockSpec(memory_space=pl.ANY)
+    hbm = pl.BlockSpec(memory_space=pltpu.HBM)
     smem = pl.BlockSpec(memory_space=pltpu.SMEM)
     bf16, f32 = jnp.bfloat16, jnp.float32
     dma = pltpu.SemaphoreType.DMA
     out = pl.pallas_call(
         kernel,
         out_shape=jax.ShapeDtypeStruct((STEPS, R, G), bf16),
-        in_specs=[hbm, smem, smem, smem, hbm, hbm, hbm],
+        in_specs=[hbm, hbm, hbm, hbm, hbm, hbm, hbm],
         out_specs=pl.BlockSpec(memory_space=pltpu.VMEM),
         scratch_shapes=[
+            pltpu.SMEM((TILES,), jnp.int32),
+            pltpu.SMEM((TILES,), jnp.int32),
+            pltpu.SMEM((TILES,), jnp.int32),
             pltpu.VMEM((TILES, TAPS, G, G), bf16),
             pltpu.VMEM((NO, HIST, R, G), bf16),
             pltpu.VMEM((STEPS, R, G), bf16),
@@ -196,7 +203,7 @@
             pltpu.VMEM((STEPS, NEAR, R, G), bf16),
             pltpu.VMEM((STEPS, NEAR, R, G), bf16),
             pltpu.VMEM((NO, R, G), bf16),
-            dma((2,)),
+            dma((5,)),
             dma((NO,)),
             dma((TILES,)),
             dma((STEPS, CHUNKS, NY - 1)),
@@ -206,16 +213,16 @@
             dma((NO - 1,)),
             dma((NO - 1,)),
         ],
-        compiler_params=pltpu.CompilerParams(collective_id=0, has_side_effects=True),
+        compiler_params=pltpu.CompilerParams(collective_id=0, vmem_limit_bytes=14680064, has_side_effects=True),
         name="march",
     )(
-        tiles.reshape(TILES, TAPS, G, G),
-        tile_src.reshape(TILES),
-        tile_obs.reshape(TILES),
-        tile_off.reshape(TILES),
-        history.reshape(NO, HIST, R, G),
-        excitation.reshape(STEPS, R, G),
-        inverse.reshape(G, G),
+        pltpu.with_memory_space_constraint(tiles.reshape(TILES, TAPS, G, G), pltpu.HBM),
+        pltpu.with_memory_space_constraint(tile_src.reshape(TILES), pltpu.HBM),
+        pltpu.with_memory_space_constraint(tile_obs.reshape(TILES), pltpu.HBM),
+        pltpu.with_memory_space_constraint(tile_off.reshape(TILES), pltpu.HBM),
+        pltpu.with_memory_space_constraint(history.reshape(NO, HIST, R, G), pltpu.HBM),
+        pltpu.with_memory_space_constraint(excitation.reshape(STEPS, R, G), pltpu.HBM),
+        pltpu.with_memory_space_constraint(inverse.reshape(G, G), pltpu.HBM),
     )
     return out.reshape(STEPS, 1, 1, 1, R, G)
 

time: 33.4 us -> 31.5 us (0.943)
  Pallas kernels: 31.9 us -> 30.6 us
  local copies, waits for them, and re-layouts: 1.32 us -> 0.61 us
    pallas_call x1, Pallas kernels: 31.9 us -> 30.6 us  [local(): pl.pallas_call(kernel, out_shape=jax.ShapeDtypeStruct((STEPS, R, G), bf16...]
    unnamed x1, local copies, waits for them, and re-layouts: 1.32 us -> 0.61 us
where the time goes in v2:
time: 31.5 us; the launch traced here: 31.2 us
  Pallas kernels  30.6 us (97%)
  local copies, waits for them, and re-layouts  0.61 us (2%)
    pallas_call x1, Pallas kernels, local(): pl.pallas_call(kernel, out_shape=jax.ShapeDtypeStruct((STEPS, R, G), bf16...  30.6 us

profile of v2, /device:TPU:32, one launch (start us, length us, event | category | flops | bytes accessed | tf_op | source)
XLA Modules:
  0.0 31.2 jit_solution(8374041934786289849)
XLA Ops:
  0.0 30.6 %march.1 = bf16[2,32,128]{2,1,0:T(8,128)(2,1)S(1)} custom-call(bf16[8,8,128,128]{3,2,1,0:T(8,128)(2,1)} %bitcast.12, s32[8]{0:T(128)} %bitcast.15, s32[8]{0:T(128)} %bitcast.16, s32[8]{0:T(128)} %bitcast.17, bf16[8,40,32,128]{3,2,1,0:T(8,128)(2,1)} %bitcast.11, bf16[2,32,128]{2,1,0:T(8,128)(2,1)} %bitcast.14, bf16[128,128]{1,0:T(8,128)(2,1)} %bitcast.13), custom_call_target="tpu_custom_call" | custom-call | tf_op jit(solution)/shard_map/march/pallas_call | solution.py:186
  30.6 0.6 %copy.10 = bf16[2,1,1,1,32,128]{5,4,3,2,1,0:T(8,128)(2,1)} copy(bf16[2,1,1,1,32,128]{5,4,3,2,1,0:T(8,128)(2,1)S(1)} %bitcast.10) | data formatting | bytes 32768

commit v3 on v2

--- a/solution.py
+++ b/solution.py
@@ -20,14 +20,17 @@
 PER = 2
 CHUNKS = NZ // PER
 NEAR = NZ - 1
+Y_BLOCKS = (NY - 1) * NZ
+SENT = Y_BLOCKS + NEAR
+NEWS = STEPS * SENT
 Y_ORDER = (2, 1, 3)
 O_ORDER = (4, 5, 2, 3, 6, 7, 1)
 
 
 def kernel(
     tiles_hbm, src_hbm, obs_hbm, off_hbm, hist_hbm, exc_hbm, inv_hbm, out_ref,
-    src_ref, obs_ref, off_ref, tiles, hist, exc, inv, contrib, part, mine, y_in, z_out, z_in, news,
-    load_sem, hist_sem, tile_sem, y_send, y_recv, z_send, z_recv, o_send, o_recv,
+    src_ref, obs_ref, off_ref, tiles, hist, exc, inv, contrib, sent, mine, y_in, z_in, news,
+    load_sem, send_sem, y_recv, z_recv, o_recv,
 ):
     src = lax.axis_index("src")
     obs = lax.axis_index("obs")
@@ -48,10 +51,8 @@
         pltpu.make_async_copy(obs_hbm, obs_ref, load_sem.at[3]),
         pltpu.make_async_copy(off_hbm, off_ref, load_sem.at[4]),
     ]
-    for j in range(NO):
-        loads.append(pltpu.make_async_copy(hist_hbm.at[j], hist.at[j], hist_sem.at[j]))
-    for t in range(TILES):
-        loads.append(pltpu.make_async_copy(tiles_hbm.at[t], tiles.at[t], tile_sem.at[t]))
+    loads.append(pltpu.make_async_copy(hist_hbm, hist, load_sem.at[5]))
+    loads.append(pltpu.make_async_copy(tiles_hbm, tiles, load_sem.at[6]))
     loads.append(pltpu.make_async_copy(exc_hbm, exc, load_sem.at[0]))
     loads.append(pltpu.make_async_copy(inv_hbm, inv, load_sem.at[1]))
     for load in loads:
@@ -78,36 +79,44 @@
 
     pl.semaphore_wait(barrier, NEAR + NY - 1 + NO - 1)
 
-    def y_copy(step, chunk, d):
-        span = pl.ds(chunk * PER, PER)
-        return pltpu.make_async_remote_copy(
-            src_ref=part.at[step, d - 1, span],
-            dst_ref=y_in.at[step, d - 1, span],
-            send_sem=y_send.at[step, chunk, d - 1],
-            recv_sem=y_recv.at[step, chunk, d - 1],
+    def y_slot(step, chunk, d):
+        return step * SENT + (chunk * (NY - 1) + d - 1) * PER
+
+    def z_slot(step, k):
+        return step * SENT + Y_BLOCKS + k
+
+    def send_y(step, chunk, d):
+        pltpu.make_async_remote_copy(
+            src_ref=sent.at[pl.ds(y_slot(step, chunk, d), PER)],
+            dst_ref=y_in.at[step, chunk, d - 1],
+            send_sem=send_sem,
+            recv_sem=y_recv.at[step, chunk],
             device_id={"src": y_peer(d)},
             device_id_type=MESH,
-        )
-
-    def z_copy(step, k):
-        return pltpu.make_async_remote_copy(
-            src_ref=z_out.at[step, k],
+        ).start()
+
+    def send_z(step, k):
+        pltpu.make_async_remote_copy(
+            src_ref=sent.at[z_slot(step, k)],
             dst_ref=z_in.at[step, k],
-            send_sem=z_send.at[step, k],
-            recv_sem=z_recv.at[step, k],
+            send_sem=send_sem,
+            recv_sem=z_recv.at[step],
             device_id={"src": z_peer(k)},
             device_id_type=MESH,
-        )
-
-    def o_copy(e):
-        return pltpu.make_async_remote_copy(
-            src_ref=news.at[obs],
+        ).start()
+
+    def send_o(e):
+        pltpu.make_async_remote_copy(
+            src_ref=sent.at[NEWS],
             dst_ref=news.at[obs],
-            send_sem=o_send.at[e - 1],
-            recv_sem=o_recv.at[e - 1],
+            send_sem=send_sem,
+            recv_sem=o_recv,
             device_id={"obs": o_peer(e)},
             device_id_type=MESH,
-        )
+        ).start()
+
+    def wait_all(ref, sem):
+        pltpu.make_async_copy(ref, ref, sem).wait()
 
     def owned_sum(step, owner):
         total = jnp.where(obs_ref[0] == owner, contrib[step, 0], 0.0)
@@ -118,26 +127,26 @@
     def scatter(step):
         for chunk in range(CHUNKS):
             for d in Y_ORDER:
-                for k in range(chunk * PER, chunk * PER + PER):
-                    owner = lax.rem(z + DELTA[k], NZ) * NY + lax.rem(y + d, NY)
-                    part[step, d - 1, k] = owned_sum(step, owner).astype(jnp.bfloat16)
-                y_copy(step, chunk, d).start()
+                for i in range(PER):
+                    owner = lax.rem(z + DELTA[chunk * PER + i], NZ) * NY + lax.rem(y + d, NY)
+                    sent[y_slot(step, chunk, d) + i] = owned_sum(step, owner).astype(jnp.bfloat16)
+                send_y(step, chunk, d)
         for k in range(NZ):
             mine[step, k] = owned_sum(step, lax.rem(z + DELTA[k], NZ) * NY + y)
 
     def gather_sum(step):
         for chunk in range(CHUNKS):
-            for d in Y_ORDER:
-                y_copy(step, chunk, d).wait_recv()
-            for k in range(chunk * PER, chunk * PER + PER):
+            wait_all(y_in.at[step, chunk], y_recv.at[step, chunk])
+            for i in range(PER):
+                k = chunk * PER + i
                 total = mine[step, k]
                 for d in Y_ORDER:
-                    total = total + y_in[step, d - 1, k].astype(jnp.float32)
+                    total = total + y_in[step, chunk, d - 1, i].astype(jnp.float32)
                 if k < NEAR:
-                    z_out[step, k] = total.astype(jnp.bfloat16)
-                    z_copy(step, k).start()
-        for k in range(NEAR - 1, -1, -1):
-            z_copy(step, k).wait_recv()
+                    sent[z_slot(step, k)] = total.astype(jnp.bfloat16)
+                    send_z(step, k)
+        wait_all(z_in.at[step], z_recv.at[step])
+        for k in range(NEAR):
             total = total + z_in[step, k].astype(jnp.float32)
         return total
 
@@ -156,11 +165,12 @@
         wide = jnp.concatenate([before] + [seen[p] for p in range(TAPS - 1)], axis=1)
         contrib[1, t] = jnp.dot(wide, block(t), preferred_element_type=jnp.float32)
 
-    news[obs] = solve(0, gather_sum(0))
+    newer = solve(0, gather_sum(0))
+    sent[NEWS] = newer
     for e in O_ORDER:
-        o_copy(e).start()
-    for e in O_ORDER:
-        o_copy(e).wait_recv()
+        send_o(e)
+    news[obs] = newer
+    wait_all(news.at[pl.ds(0, NO - 1)], o_recv)
     for t in range(TILES):
         fresh = news[src_ref[t]]
         fresh = jnp.where(off_ref[t] == 0, fresh, jnp.zeros_like(fresh))
@@ -168,14 +178,7 @@
     scatter(1)
     solve(1, gather_sum(1))
 
-    for step in range(STEPS):
-        for chunk in range(CHUNKS):
-            for d in Y_ORDER:
-                y_copy(step, chunk, d).wait_send()
-        for k in range(NEAR):
-            z_copy(step, k).wait_send()
-    for e in O_ORDER:
-        o_copy(e).wait_send()
+    wait_all(sent, send_sem)
 
 
 def local(tiles, tile_src, tile_obs, tile_off, history, excitation, inverse):
@@ -197,21 +200,16 @@
             pltpu.VMEM((STEPS, R, G), bf16),
             pltpu.VMEM((G, G), bf16),
             pltpu.VMEM((STEPS, TILES, R, G), f32),
-            pltpu.VMEM((STEPS, NY - 1, NZ, R, G), bf16),
+            pltpu.VMEM((NEWS + NO - 1, R, G), bf16),
             pltpu.VMEM((STEPS, NZ, R, G), f32),
-            pltpu.VMEM((STEPS, NY - 1, NZ, R, G), bf16),
-            pltpu.VMEM((STEPS, NEAR, R, G), bf16),
+            pltpu.VMEM((STEPS, CHUNKS, NY - 1, PER, R, G), bf16),
             pltpu.VMEM((STEPS, NEAR, R, G), bf16),
             pltpu.VMEM((NO, R, G), bf16),
-            dma((5,)),
-            dma((NO,)),
-            dma((TILES,)),
-            dma((STEPS, CHUNKS, NY - 1)),
-            dma((STEPS, CHUNKS, NY - 1)),
-            dma((STEPS, NEAR)),
-            dma((STEPS, NEAR)),
-            dma((NO - 1,)),
-            dma((NO - 1,)),
+            dma((7,)),
+            dma(()),
+            dma((STEPS, CHUNKS)),
+            dma((STEPS,)),
+            dma(()),
         ],
         compiler_params=pltpu.CompilerParams(collective_id=0, vmem_limit_bytes=14680064, has_side_effects=True),
         name="march",

time: 31.5 us -> 30.3 us (0.962)
  Pallas kernels: 30.6 us -> 29.6 us
    pallas_call x1, Pallas kernels: 30.6 us -> 29.6 us  [local(): pl.pallas_call(kernel, out_shape=jax.ShapeDtypeStruct((STEPS, R, G), bf16...]
where the time goes in v3:
time: 30.3 us; the launch traced here: 30.2 us
  Pallas kernels  29.6 us (98%)
  local copies, waits for them, and re-layouts  0.61 us (2%)
    pallas_call x1, Pallas kernels, local(): pl.pallas_call(kernel, out_shape=jax.ShapeDtypeStruct((STEPS, R, G), bf16...  29.6 us
    unnamed x1, local copies, waits for them, and re-layouts  0.61 us

profile of v3, /device:TPU:32, one launch (start us, length us, event | category | flops | bytes accessed | tf_op | source)
XLA Modules:
  0.0 30.2 jit_solution(16818504440569776983)
XLA Ops:
  0.0 29.6 %march.1 = bf16[2,32,128]{2,1,0:T(8,128)(2,1)S(1)} custom-call(bf16[8,8,128,128]{3,2,1,0:T(8,128)(2,1)} %bitcast.12, s32[8]{0:T(128)} %bitcast.15, s32[8]{0:T(128)} %bitcast.16, s32[8]{0:T(128)} %bitcast.17, bf16[8,40,32,128]{3,2,1,0:T(8,128)(2,1)} %bitcast.11, bf16[2,32,128]{2,1,0:T(8,128)(2,1)} %bitcast.14, bf16[128,128]{1,0:T(8,128)(2,1)} %bitcast.13), custom_call_target="tpu_custom_call" | custom-call | tf_op jit(solution)/shard_map/march/pallas_call | solution.py:189
  29.6 0.6 %copy.10 = bf16[2,1,1,1,32,128]{5,4,3,2,1,0:T(8,128)(2,1)} copy(bf16[2,1,1,1,32,128]{5,4,3,2,1,0:T(8,128)(2,1)S(1)} %bitcast.10) | data formatting | bytes 32768
